TPU v7x, 32 devices: a whole 2x2x4 slice. The times are simulated.
32 devices in a mesh: outer: 8 (over z, x), inner: 4 (over y, core).
Axes of the slice: x: 2, y: 2, z: 4, core: 2. Of those that a mesh axis runs over, the one named last changes fastest.
Arguments:
- state_vector: float32 [2, 8, 4, 32768], P(None, 'outer', 'inner'), may hold values from -6 to 6
- gate_matrices: float32 [4, 2, 128, 128], replicated, may hold values from -4 to 4, as said below
Outputs:
- final_state: float32 [2, 8, 4, 32768], P(None, 'outer', 'inner')
- state_rms: float32 [], replicated
Inputs may be any that keep to these rules, and one draw needn't show every extreme that they name: `gate_matrices`: each gate is a general complex matrix, not necessarily unitary.
All inputs are finite; a program needn't handle non-finite values.
Results may differ from a plain program's by a relative error of at most 0.000098.
Values sent between devices are 32-bit elements; how exact they have to be, the bound alone decides.
A program may use at most 64 MiB of HBM per device.

v0:
```python
import functools

import jax
import jax.numpy as jnp
from jax import lax
from jax.experimental import pallas as pl
from jax.experimental.pallas import tpu as pltpu
from jax.sharding import PartitionSpec as P

MESH = pl.DeviceIdType.MESH
TRADE_LIMIT = 56_150_000
LIMIT = 16 * 1024 * 1024


def halves(values):
    high = values.astype(jnp.bfloat16)
    low = (values - high.astype(jnp.float32)).astype(jnp.bfloat16)
    return high, low


def product(left, right, dims):
    def one(a, b):
        return lax.dot_general(a, b, (dims, ((), ())), preferred_element_type=jnp.float32)

    return one(left[0], right[0]) + (one(left[0], right[1]) + one(left[1], right[0]))


def complex_matrix(real, imag):
    top = jnp.concatenate([real, -imag], axis=1)
    bottom = jnp.concatenate([imag, real], axis=1)
    return halves(jnp.concatenate([top, bottom], axis=0))


def spread(position, count):
    half, rest = count // 2, position // 2
    return (position % 2) * half + (rest % 2) * (half // 2) + rest // 2


def kernel(
    n_outer, n_inner, chunks, state_in, gates_in, held_c, sums,
    state, gates, sent_a, held_a, sent_b, held_b, sent_c, part, fetched,
    send_a, recv_a, send_b, recv_b, send_c, recv_c, send_s, recv_s,
):
    def fetch(at):
        if at == 0:
            return pltpu.make_async_copy(state_in, state, fetched.at[0])
        return pltpu.make_async_copy(gates_in.at[at - 1], gates.at[at - 1], fetched.at[at])

    for at in (0, 1, 4, 2, 3):
        fetch(at).start()
    dim = gates.shape[2]
    passive = state.shape[1] // dim
    sub = passive // chunks
    step = dim // chunks
    rows_outer = dim // n_outer * sub
    rows_inner = dim // n_inner * sub
    ratio = n_outer // n_inner
    n_all = n_outer * n_inner
    outer, inner = lax.axis_index("outer"), lax.axis_index("inner")
    me = outer * n_inner + inner

    def block(ref, chunk, at, rows):
        return ref.at[chunk, :, pl.ds(pl.multiple_of(at * rows, rows), rows), :]

    def remote(src, dst, send, recv, target):
        return pltpu.make_async_remote_copy(
            src_ref=src, dst_ref=dst, send_sem=send, recv_sem=recv,
            device_id=target, device_id_type=MESH,
        )

    far_first = sorted(range(n_outer), key=lambda k: abs(2 * k - n_outer))

    def everyone(act):
        if n_all > 64:

            def body(k, carry):
                one(act, k // n_inner, k % n_inner)
                return carry

            lax.fori_loop(1, n_all, body, 0)
            return
        for a in far_first:
            for b in range(n_inner):
                if a or b:
                    one(act, a, b)

    def one(act, a, b):
        ahead = ((outer + a) % n_outer, (inner + b) % n_inner)
        behind = ((outer + n_outer - a) % n_outer, (inner + n_inner - b) % n_inner)
        act(a * n_inner + b, ahead, behind)

    barrier = pltpu.get_barrier_semaphore()

    for k in range(1, n_outer):
        pl.semaphore_signal(
            barrier, inc=1, device_id=((outer + k) % n_outer, inner), device_id_type=MESH
        )
    for k in range(1, n_inner):
        pl.semaphore_signal(
            barrier, inc=1, device_id=(outer, (inner + k) % n_inner), device_id_type=MESH
        )

    def load(ref, chunk):
        return jnp.concatenate(
            [
                jnp.concatenate(
                    [ref[chunk, c, pl.ds(b, dim, stride=sub), :] for b in range(sub)], axis=1
                )
                for c in range(2)
            ],
            axis=0,
        )

    def store(ref, chunk, values):
        for c in range(2):
            for b in range(sub):
                ref[chunk, c, pl.ds(b, dim, stride=sub), :] = values[
                    c * dim : (c + 1) * dim, b * dim : (b + 1) * dim
                ]

    def low_gate(values):
        rows = values.shape[0] // 2
        matrix = complex_matrix(gates[3, 0], gates[3, 1])
        columns = []
        for b in range(values.shape[1] // dim):
            both = values[:, b * dim : (b + 1) * dim]
            wide = jnp.concatenate([both[:rows], both[rows:]], axis=1)
            wide = product(halves(wide), matrix, ((1,), (1,)))
            columns.append(jnp.concatenate([wide[:, :dim], wide[:, dim:]], axis=0))
        return jnp.concatenate(columns, axis=1)

    fetch(0).wait()
    fetch(1).wait()
    first = halves(
        jnp.concatenate(
            [
                jnp.concatenate(
                    [state[c, w * dim : (w + 1) * dim, :] for w in range(passive)], axis=1
                )
                for c in range(2)
            ],
            axis=0,
        )
    )

    def trade_a(chunk):
        for k in far_first[:-1]:
            to = (outer + k) % n_outer
            remote(
                block(sent_a, chunk, spread(to, n_outer), rows_outer),
                block(held_a, chunk, outer, rows_outer),
                send_a.at[chunk, to], recv_a.at[chunk, outer], (to, inner),
            ).start()
        pltpu.make_async_copy(
            block(sent_a, chunk, spread(outer, n_outer), rows_outer),
            block(held_a, chunk, outer, rows_outer),
            recv_a.at[chunk, outer],
        ).start()

    for chunk in range(chunks):
        pick = pl.ds(chunk, step, stride=chunks)
        matrix = complex_matrix(gates[0, 0, pick, :], gates[0, 1, pick, :])
        values = product(matrix, first, ((1,), (0,)))
        if chunk > 0:
            if chunk == 1:
                fetch(4).wait()
            values = low_gate(values)
        for c in range(2):
            for w in range(passive):
                sent_a[chunk, c, w * step : (w + 1) * step, :] = values[
                    c * step : (c + 1) * step, w * dim : (w + 1) * dim
                ]
        if chunk == 0:
            pl.semaphore_wait(barrier, n_outer + n_inner - 2)
        trade_a(chunk)

    fetch(2).wait()
    matrix = complex_matrix(gates[1, 0], gates[1, 1])
    mine = spread(outer, n_outer)
    column, within = mine // ratio, mine % ratio
    slot = inner * ratio + within
    for chunk in range(chunks):
        for k in range(n_outer):
            spot = block(held_a, chunk, k, rows_outer)
            remote(spot, spot, send_a.at[chunk, k], recv_a.at[chunk, k], (outer, inner)).wait_recv()
        values = halves(load(held_a, chunk))
        store(sent_b, chunk, product(matrix, values, ((1,), (0,))))
        for k in far_first:
            to = (outer + k) % n_outer
            src = block(sent_b, chunk, to, rows_outer)
            dst = block(held_b, chunk, slot, rows_outer)
            copy = remote(
                src, dst, send_b.at[chunk, to], recv_b.at[chunk, slot], (to, column)
            )
            if k > 0:
                copy.start()
            else:
                pl.when(column != inner)(copy.start)
                pl.when(column == inner)(
                    pltpu.make_async_copy(src, dst, recv_b.at[chunk, slot]).start
                )

    fetch(3).wait()
    matrix = complex_matrix(gates[2, 0], gates[2, 1])
    total = jnp.zeros((1, dim), jnp.float32)
    own = pltpu.make_async_copy(part, sums.at[me], recv_s.at[0])

    def share(k, ahead, behind):
        remote(part, sums.at[me], send_s.at[k], recv_s.at[k], ahead).start()

    for chunk in range(chunks):
        for k in range(n_outer):
            spot = block(held_b, chunk, k, rows_outer)
            remote(spot, spot, send_b.at[chunk, k], recv_b.at[chunk, k], (outer, inner)).wait_recv()
        values = product(matrix, halves(load(held_b, chunk)), ((1,), (0,)))
        if chunk == 0:
            if chunks == 1:
                fetch(4).wait()
            values = low_gate(values)
        for b in range(sub):
            piece = values[:, b * dim : (b + 1) * dim]
            total = total + jnp.sum(piece * piece, axis=0, keepdims=True)
        if chunk == chunks - 1:
            part[...] = total
            everyone(share)
            own.start()
        store(sent_c, chunk, values)
        for k in range(1, n_inner):
            to = (inner + k) % n_inner
            remote(
                block(sent_c, chunk, to, rows_inner),
                block(held_c, chunk, inner, rows_inner),
                send_c.at[chunk, to], recv_c.at[chunk, inner], (outer, to),
            ).start()
        pltpu.make_async_copy(
            block(sent_c, chunk, inner, rows_inner),
            block(held_c, chunk, inner, rows_inner),
            recv_c.at[chunk, inner],
        ).start()

    def arrived(k, ahead, behind):
        spot = sums.at[behind[0] * n_inner + behind[1]]
        remote(part, spot, send_s.at[k], recv_s.at[k], ahead).wait_recv()

    def left(k, ahead, behind):
        remote(part, sums.at[me], send_s.at[k], recv_s.at[k], ahead).wait_send()

    for chunk in range(chunks):
        for k in range(n_inner):
            spot = block(held_c, chunk, k, rows_inner)
            remote(spot, spot, send_c.at[chunk, k], recv_c.at[chunk, k], (outer, inner)).wait_recv()

    for chunk in range(chunks):
        for k in range(1, n_outer):
            to = (outer + k) % n_outer
            spot = block(sent_a, chunk, to, rows_outer)
            remote(spot, spot, send_a.at[chunk, to], recv_a.at[chunk, to], (to, inner)).wait_send()
        for k in range(n_outer):
            to = (outer + k) % n_outer
            spot = block(sent_b, chunk, to, rows_outer)
            copy = remote(spot, spot, send_b.at[chunk, to], recv_b.at[chunk, to], (to, column))
            if k > 0:
                copy.wait_send()
            else:
                pl.when(column != inner)(copy.wait_send)
        for k in range(1, n_inner):
            to = (inner + k) % n_inner
            spot = block(sent_c, chunk, to, rows_inner)
            remote(spot, spot, send_c.at[chunk, to], recv_c.at[chunk, to], (outer, to)).wait_send()
    everyone(left)
    own.wait()
    everyone(arrived)


def finish(n_all, values, sums, out, rms):
    chunks, _, rows, dim = values.shape
    whole = jnp.sum(jnp.sum(sums[...], axis=0), axis=1, keepdims=True)
    root = jnp.sqrt(whole / (n_all * chunks * rows * dim))
    rms[...] = root
    scale = jnp.broadcast_to(1.0 / root, (8, dim))
    for chunk in range(chunks):
        for c in range(2):
            scaled = values[chunk, c].reshape(-1, 8, dim) * scale[None]
            out[c, pl.ds(chunk, rows, stride=chunks), :] = scaled.reshape(-1, dim)


def shards(n_outer, n_inner, state_vector, gate_matrices):
    dim = gate_matrices.shape[2]
    amp_count = state_vector.shape[3]
    rows = amp_count // dim
    passive = rows // dim
    chunks = passive if (dim // n_outer) % 8 == 0 else 1
    held = pltpu.VMEM((chunks, 2, rows // chunks, dim), jnp.float32)
    n_all = n_outer * n_inner
    dma = pltpu.SemaphoreType.DMA
    vmem = pl.BlockSpec(memory_space=pltpu.VMEM)
    hbm = pl.BlockSpec(memory_space=pltpu.HBM)
    anywhere = pl.BlockSpec(memory_space=pl.ANY)
    values, sums = pl.pallas_call(
        functools.partial(kernel, n_outer, n_inner, chunks),
        out_shape=(
            jax.ShapeDtypeStruct((chunks, 2, rows // chunks, dim), jnp.float32),
            jax.ShapeDtypeStruct((n_all, 1, dim), jnp.float32),
        ),
        in_specs=[hbm, hbm],
        out_specs=(anywhere, anywhere),
        scratch_shapes=[
            pltpu.VMEM((2, rows, dim), jnp.float32),
            pltpu.VMEM(gate_matrices.shape, jnp.float32),
        ]
        + [held] * 5
        + [pltpu.VMEM((1, dim), jnp.float32), dma((5,))]
        + [dma((chunks, n_outer))] * 4
        + [dma((chunks, n_inner))] * 2
        + [dma((n_all,))] * 2,
        compiler_params=pltpu.CompilerParams(
            collective_id=0, has_side_effects=True, vmem_limit_bytes=TRADE_LIMIT
        ),
    )(state_vector.reshape(2, rows, dim), gate_matrices)
    final_state, root = pl.pallas_call(
        functools.partial(finish, n_all),
        out_shape=(
            jax.ShapeDtypeStruct((2, rows, dim), jnp.float32),
            jax.ShapeDtypeStruct((1, 1), jnp.float32),
        ),
        in_specs=[vmem, vmem],
        out_specs=(vmem, vmem),
        compiler_params=pltpu.CompilerParams(vmem_limit_bytes=LIMIT),
    )(values, sums)
    return final_state.reshape(state_vector.shape), root.reshape(())


def solution(mesh):
    in_specs = (P(None, "outer", "inner", None), P())
    out_specs = (P(None, "outer", "inner", None), P())
    body = functools.partial(shards, mesh.shape["outer"], mesh.shape["inner"])
    return jax.shard_map(body, mesh=mesh, in_specs=in_specs, out_specs=out_specs, check_vma=False)
```

profile of v0, /device:TPU:0, one launch (start us, length us, event | category | flops | bytes accessed | tf_op | source)
XLA Modules:
  0.0 26.6 jit_solution(9027811969930617509)
XLA Ops:
  0.6 25.1 %shard_map.41 = (f32[2,2,128,128]{3,2,1,0:T(8,128)S(1)}, f32[32,1,128]{2,1,0:T(1,128)S(1)}) custom-call(f32[2,256,128]{2,1,0:T(8,128)} %bitcast.3, f32[4,2,128,128]{3,2,1,0:T(8,128)} %gates_in.1), custom_call_target="tpu_custom_call" | custom-call | tf_op jit(solution)/shard_map/pallas_call | solution.py:299
  25.7 0.8 %shard_map.42 = (f32[2,256,128]{2,1,0:T(8,128)}, f32[1,1]{1,0:T(1,128)}) custom-call(f32[2,2,128,128]{3,2,1,0:T(8,128)S(1)} %get-tuple-element.6.values, f32[32,1,128]{2,1,0:T(1,128)S(1)} %get-tuple-element.7.sums), custom_call_target="tpu_custom_call" | custom-call | tf_op jit(solution)/shard_map/pallas_call | solution.py:320
where the time goes:
time: 26.7 us; the launch traced here: 26.6 us
  Pallas kernels  25.9 us (97%)
  between operations  0.64 us (2%)
    pallas_call x1, Pallas kernels, shards(): pl.pallas_call(functools.partial(kernel, n_outer, n_inner, chunks), out_s...  25.1 us
    pallas_call x1, Pallas kernels, shards(): pl.pallas_call(functools.partial(finish, n_all), out_shape=(jax.ShapeDtyp...  0.85 us

commit v1 on v0

--- a/solution.py
+++ b/solution.py
@@ -330,8 +330,279 @@
     return final_state.reshape(state_vector.shape), root.reshape(())
 
 
+def relabel(tiles, names, order):
+    count = len(names)
+    places = [count - 1 - names.index(name) for name in order]
+    picked = []
+    for at in range(len(tiles)):
+        bits = [(at >> (count - 1 - j)) & 1 for j in range(count)]
+        picked.append(tiles[sum(bit << place for bit, place in zip(bits, places))])
+    return picked
+
+
+def swap(tiles, names, major, lane):
+    step = 1 << (len(names) - 1 - names.index(major))
+    lows = [at for at in range(len(tiles)) if not at & step]
+    low = jnp.concatenate([tiles[at] for at in lows], axis=0)
+    high = jnp.concatenate([tiles[at + step] for at in lows], axis=0)
+    size = low.shape[1]
+    first = lax.broadcasted_iota(jnp.int32, low.shape, 1) // lane % 2 == 0
+    new_low = jnp.where(first, low, pltpu.roll(high, lane, 1))
+    new_high = jnp.where(first, pltpu.roll(low, size - lane, 1), high)
+    out = list(tiles)
+    for j, at in enumerate(lows):
+        out[at] = new_low[j * 8 : (j + 1) * 8]
+        out[at + step] = new_high[j * 8 : (j + 1) * 8]
+    return out
+
+
+def split(values):
+    return [values[at * 8 : (at + 1) * 8] for at in range(values.shape[0] // 8)]
+
+
+def join(tiles):
+    return jnp.concatenate(tiles, axis=0)
+
+
+def rename(names, old, new):
+    return [new if name == old else name for name in names]
+
+
+def bits(name, count):
+    return [name + str(j) for j in reversed(range(count))]
+
+
+def fast_kernel(
+    n_outer, n_inner, state_in, gates_in, held_b, sums,
+    state, gates, sent_a, held_a, sent_b, part, fetched,
+    send_a, recv_a, send_b, recv_b, send_s, recv_s, own_s,
+):
+    def fetch(at):
+        if at == 0:
+            return pltpu.make_async_copy(state_in, state, fetched.at[0])
+        return pltpu.make_async_copy(gates_in.at[at - 1], gates.at[at - 1], fetched.at[at])
+
+    for at in (0, 1, 4, 2, 3):
+        fetch(at).start()
+    dim = gates.shape[2]
+    chunks = state.shape[1] // dim
+    n_all = n_outer * n_inner
+    n_bits, o_bits, i_bits = (v.bit_length() - 1 for v in (n_all, n_outer, n_inner))
+    outer, inner = lax.axis_index("outer"), lax.axis_index("inner")
+    me = outer * n_inner + inner
+
+    def peer(k):
+        a, b = outer, inner
+        for j in range(o_bits):
+            if (k // n_inner) >> j & 1:
+                a = a + (1 - 2 * (outer // 2**j % 2)) * 2**j
+        for j in range(i_bits):
+            if (k % n_inner) >> j & 1:
+                b = b + (1 - 2 * (inner // 2**j % 2)) * 2**j
+        return a, b
+
+    half = n_all // 2
+    order = []
+    for k in reversed(range(half)):
+        order += [k + half] + ([k] if k else [])
+    barrier = pltpu.get_barrier_semaphore()
+    for k in order:
+        pl.semaphore_signal(barrier, inc=1, device_id=peer(k), device_id_type=MESH)
+
+    def remote(src, dst, send, recv, target):
+        return pltpu.make_async_remote_copy(
+            src_ref=src, dst_ref=dst, send_sem=send, recv_sem=recv,
+            device_id=target, device_id_type=MESH,
+        )
+
+    def tile(ref, chunk, at):
+        return ref.at[chunk, pl.ds(pl.multiple_of(at * 8, 8), 8), :]
+
+    def trade(sent, held, send, recv, chunk):
+        for k in order:
+            a, b = peer(k)
+            remote(
+                tile(sent, chunk, a * n_inner + b), tile(held, chunk, me),
+                send.at[chunk], recv.at[chunk], (a, b),
+            ).start()
+        pltpu.make_async_copy(
+            tile(sent, chunk, me), tile(held, chunk, me), recv.at[chunk]
+        ).start()
+
+    def arrived(held, send, recv, chunk):
+        spot = held.at[chunk]
+        remote(spot, spot, send.at[chunk], recv.at[chunk], (outer, inner)).wait_recv()
+
+    def left(sent, send, recv, chunk):
+        spot = sent.at[chunk, pl.ds(0, (n_all - 1) * 8), :]
+        remote(spot, spot, send.at[chunk], recv.at[chunk], (outer, inner)).wait_send()
+
+    top = dim // 2
+    fetch(1).wait()
+
+    def rows0(c):
+        return jnp.concatenate(
+            [
+                gates[0, c, pl.ds(high * top + low, top // 2, stride=2), :]
+                for high in range(2)
+                for low in range(2)
+            ],
+            axis=0,
+        )
+
+    first = complex_matrix(rows0(0), rows0(1))
+    fetch(4).wait()
+    real, imag = gates[3, 0], gates[3, 1]
+    low = []
+    for high in range(2):
+        spot = slice(high * top, (high + 1) * top)
+        low.append(jnp.concatenate([real[spot], -imag[spot]], axis=1))
+        low.append(jnp.concatenate([imag[spot], real[spot]], axis=1))
+    low = halves(jnp.concatenate(low, axis=0))
+    fetch(0).wait()
+    for chunk in range(chunks):
+        values = jnp.concatenate(
+            [state[c, chunk * dim : (chunk + 1) * dim, :] for c in range(2)], axis=0
+        )
+        values = product(first, halves(values), ((1,), (0,)))
+        wide = jnp.concatenate([values[:dim], values[dim:]], axis=1)
+        wide = product(halves(wide), low, ((1,), (1,)))
+        tiles = split(jnp.concatenate([wide[:, :dim], wide[:, dim:]], axis=0))
+        names = ["b6", "b13", "b7", "b12", "b11"]
+        tiles = swap(tiles, names, "b12", dim // 4)
+        names = rename(names, "b12", "b5")
+        tiles = swap(tiles, names, "b11", dim // 8)
+        sent_a[chunk] = join(tiles)
+        if chunk == 0:
+            pl.semaphore_wait(barrier, n_all - 1)
+        trade(sent_a, held_a, send_a, recv_a, chunk)
+
+    fetch(2).wait()
+    second = complex_matrix(gates[1, 0], gates[1, 1])
+    fetch(3).wait()
+    third = complex_matrix(gates[2, 0], gates[2, 1])
+    o_names, i_names = bits("o", o_bits), bits("i", i_bits)
+    total = jnp.zeros((1, dim), jnp.float32)
+    for chunk in range(chunks):
+        arrived(held_a, send_a, recv_a, chunk)
+        tiles = split(held_a[chunk])
+        names = o_names + i_names
+        tiles = swap(tiles, names, "i1", dim // 2)
+        names = rename(names, "i1", "c")
+        tiles = swap(tiles, names, "i0", dim // 8)
+        names = rename(names, "i0", "b11")
+        rows = ["c"] + o_names + ["b11"]
+        values = product(second, halves(join(relabel(tiles, names, rows))), ((1,), (0,)))
+        tiles, names = split(values), rows
+        for name, new, lane in (("o2", "i1", 2), ("o1", "b12", 4), ("o0", "i0", 8)):
+            tiles = swap(tiles, names, name, dim // lane)
+            names = rename(names, name, new)
+        rows = ["c"] + i_names + ["b12", "b11"]
+        values = product(third, halves(join(relabel(tiles, names, rows))), ((1,), (0,)))
+        total = total + jnp.sum(values * values, axis=0, keepdims=True)
+        if chunk == chunks - 1:
+            part[...] = total
+            for k in order:
+                remote(part, sums.at[me], send_s, recv_s, peer(k)).start()
+            pltpu.make_async_copy(part, sums.at[me], own_s).start()
+        tiles, names = split(values), rows
+        for name, new, lane in (("c", "o2", 2), ("b12", "o1", 4), ("b11", "o0", 8)):
+            tiles = swap(tiles, names, name, dim // lane)
+            names = rename(names, name, new)
+        sent_b[chunk] = join(relabel(tiles, names, o_names + i_names))
+        trade(sent_b, held_b, send_b, recv_b, chunk)
+
+    for chunk in range(chunks):
+        left(sent_a, send_a, recv_a, chunk)
+    everyone = sums.at[pl.ds(0, n_all - 1)]
+    remote(everyone, everyone, send_s, recv_s, (outer, inner)).wait()
+    pltpu.make_async_copy(part, sums.at[me], own_s).wait()
+    for chunk in range(chunks):
+        arrived(held_b, send_b, recv_b, chunk)
+        left(sent_b, send_b, recv_b, chunk)
+
+
+def fast_finish(n_all, values, sums, out, rms):
+    chunks, rows, dim = values.shape
+    half = rows // 2
+    whole = jnp.sum(jnp.sum(sums[...], axis=0), axis=1, keepdims=True)
+    root = jnp.sqrt(whole / (n_all * chunks * half * dim))
+    rms[...] = root
+    scale = jnp.broadcast_to(1.0 / root, (8, dim))
+    for chunk in range(chunks):
+        tiles = split(values[chunk])
+        names = ["b6", "b13", "b7", "b5", "b4"]
+        for name, new, lane in (("b6", "c", 2), ("b5", "b12", 4), ("b4", "b11", 8)):
+            tiles = swap(tiles, names, name, dim // lane)
+            names = rename(names, name, new)
+        tiles = relabel(tiles, names, ["c", "b13", "b12", "b11", "b7"])
+        for at in range(len(tiles)):
+            c, rest = divmod(at, len(tiles) // 2)
+            start = chunk * half + rest // 2 * 16 + rest % 2
+            out[c, pl.ds(start, 8, stride=2), :] = tiles[at] * scale
+
+
+def fast_shards(n_outer, n_inner, state_vector, gate_matrices):
+    dim = gate_matrices.shape[2]
+    rows = state_vector.shape[3] // dim
+    chunks = rows // dim
+    n_all = n_outer * n_inner
+    held = pltpu.VMEM((chunks, n_all * 8, dim), jnp.float32)
+    dma = pltpu.SemaphoreType.DMA
+    vmem = pl.BlockSpec(memory_space=pltpu.VMEM)
+    hbm = pl.BlockSpec(memory_space=pltpu.HBM)
+    anywhere = pl.BlockSpec(memory_space=pl.ANY)
+    values, sums = pl.pallas_call(
+        functools.partial(fast_kernel, n_outer, n_inner),
+        out_shape=(
+            jax.ShapeDtypeStruct((chunks, n_all * 8, dim), jnp.float32),
+            jax.ShapeDtypeStruct((n_all, 1, dim), jnp.float32),
+        ),
+        in_specs=[hbm, hbm],
+        out_specs=(anywhere, anywhere),
+        scratch_shapes=[
+            pltpu.VMEM((2, rows, dim), jnp.float32),
+            pltpu.VMEM(gate_matrices.shape, jnp.float32),
+        ]
+        + [held] * 3
+        + [pltpu.VMEM((1, dim), jnp.float32), dma((5,))]
+        + [dma((chunks,))] * 4
+        + [dma(())] * 3,
+        compiler_params=pltpu.CompilerParams(
+            collective_id=0, has_side_effects=True, vmem_limit_bytes=TRADE_LIMIT
+        ),
+    )(state_vector.reshape(2, rows, dim), gate_matrices)
+    final_state, root = pl.pallas_call(
+        functools.partial(fast_finish, n_all),
+        out_shape=(
+            jax.ShapeDtypeStruct((2, rows, dim), jnp.float32),
+            jax.ShapeDtypeStruct((1, 1), jnp.float32),
+        ),
+        in_specs=[vmem, vmem],
+        out_specs=(vmem, vmem),
+        compiler_params=pltpu.CompilerParams(vmem_limit_bytes=LIMIT),
+    )(values, sums)
+    return final_state.reshape(state_vector.shape), root.reshape(())
+
+
+def fits(n_outer, n_inner, state_vector, gate_matrices):
+    dim = gate_matrices.shape[2]
+    rows = state_vector.shape[3] // dim
+    return (
+        rows == 2 * dim
+        and n_outer * n_inner * 8 == 2 * dim
+        and dim == n_outer * 16
+        and dim == n_inner * 32
+    )
+
+
+def shards_of(n_outer, n_inner, state_vector, gate_matrices):
+    run = fast_shards if fits(n_outer, n_inner, state_vector, gate_matrices) else shards
+    return run(n_outer, n_inner, state_vector, gate_matrices)
+
+
 def solution(mesh):
     in_specs = (P(None, "outer", "inner", None), P())
     out_specs = (P(None, "outer", "inner", None), P())
-    body = functools.partial(shards, mesh.shape["outer"], mesh.shape["inner"])
+    body = functools.partial(shards_of, mesh.shape["outer"], mesh.shape["inner"])
     return jax.shard_map(body, mesh=mesh, in_specs=in_specs, out_specs=out_specs, check_vma=False)

time: 26.7 us -> 24.5 us (0.918)
  Pallas kernels: 25.9 us -> 23.7 us
    pallas_call x2, Pallas kernels: 25.9 us -> 23.7 us  [the longest x1 22.6 us: fast_shards(): pl.pallas_call(functools.partial(fast_kernel, n_outer, n_inner), out_shap...]
where the time goes in v1:
time: 24.5 us; the launch traced here: 24.4 us
  Pallas kernels  23.7 us (97%)
  between operations  0.64 us (3%)
    pallas_call x1, Pallas kernels, fast_shards(): pl.pallas_call(functools.partial(fast_kernel, n_outer, n_inner), out_shap...  22.6 us
    pallas_call x1, Pallas kernels, fast_shards(): pl.pallas_call(functools.partial(fast_finish, n_all), out_shape=(jax.Shap...  1.1 us

profile of v1, /device:TPU:0, one launch (start us, length us, event | category | flops | bytes accessed | tf_op | source)
XLA Modules:
  0.0 24.4 jit_solution(6323415253538893191)
XLA Ops:
  0.6 22.6 %shard_map.41 = (f32[2,256,128]{2,1,0:T(8,128)S(1)}, f32[32,1,128]{2,1,0:T(1,128)S(1)}) custom-call(f32[2,256,128]{2,1,0:T(8,128)} %bitcast.3, f32[4,2,128,128]{3,2,1,0:T(8,128)} %gates_in.1), custom_call_target="tpu_custom_call" | custom-call | tf_op jit(solution)/shard_map/pallas_call | solution.py:555
  23.3 1.1 %shard_map.42 = (f32[2,256,128]{2,1,0:T(8,128)}, f32[1,1]{1,0:T(1,128)}) custom-call(f32[2,256,128]{2,1,0:T(8,128)S(1)} %get-tuple-element.6.values, f32[32,1,128]{2,1,0:T(1,128)S(1)} %get-tuple-element.7.sums), custom_call_target="tpu_custom_call" | custom-call | tf_op jit(solution)/shard_map/pallas_call | solution.py:575

commit v2 on v1

--- a/solution.py
+++ b/solution.py
@@ -382,32 +382,40 @@
             return pltpu.make_async_copy(state_in, state, fetched.at[0])
         return pltpu.make_async_copy(gates_in.at[at - 1], gates.at[at - 1], fetched.at[at])
 
-    for at in (0, 1, 4, 2, 3):
-        fetch(at).start()
     dim = gates.shape[2]
     chunks = state.shape[1] // dim
     n_all = n_outer * n_inner
-    n_bits, o_bits, i_bits = (v.bit_length() - 1 for v in (n_all, n_outer, n_inner))
+    o_bits, i_bits = n_outer.bit_length() - 1, n_inner.bit_length() - 1
     outer, inner = lax.axis_index("outer"), lax.axis_index("inner")
     me = outer * n_inner + inner
 
+    plane = 2 * n_inner
+    levels = n_all // plane
+    span = levels // 2
+    level, spot = me // plane, me % plane
+    side = level // span
+
     def peer(k):
-        a, b = outer, inner
-        for j in range(o_bits):
-            if (k // n_inner) >> j & 1:
-                a = a + (1 - 2 * (outer // 2**j % 2)) * 2**j
-        for j in range(i_bits):
-            if (k % n_inner) >> j & 1:
-                b = b + (1 - 2 * (inner // 2**j % 2)) * 2**j
-        return a, b
-
-    half = n_all // 2
-    order = []
-    for k in reversed(range(half)):
-        order += [k + half] + ([k] if k else [])
+        j, p = k
+        if j < span:
+            to = (1 - side) * (levels - 1 - j) + side * j
+        else:
+            to = side * span + (level + j) % span
+        to = to * plane + spot
+        for q in range(i_bits + 1):
+            if p >> q & 1:
+                to = to + (1 - 2 * (spot // 2**q % 2)) * 2**q
+        return to // n_inner, to % n_inner
+
+    spots = sorted(range(plane), key=lambda p: (-p.bit_count(), -p))
+    across = [(j, p) for j in range(span) for p in spots]
+    beside = [(j, p) for j in reversed(range(span, levels)) for p in spots][:-1]
+    order = [k for both in zip(across, beside) for k in both] + across[-1:]
     barrier = pltpu.get_barrier_semaphore()
-    for k in order:
+    for k in across + beside:
         pl.semaphore_signal(barrier, inc=1, device_id=peer(k), device_id_type=MESH)
+    for at in (0, 1, 4, 2, 3):
+        fetch(at).start()
 
     def remote(src, dst, send, recv, target):
         return pltpu.make_async_remote_copy(
@@ -418,24 +426,26 @@
     def tile(ref, chunk, at):
         return ref.at[chunk, pl.ds(pl.multiple_of(at * 8, 8), 8), :]
 
-    def trade(sent, held, send, recv, chunk):
-        for k in order:
+    def trade(sent, held, send, recv, chunk, peers):
+        for k in peers:
             a, b = peer(k)
             remote(
                 tile(sent, chunk, a * n_inner + b), tile(held, chunk, me),
                 send.at[chunk], recv.at[chunk], (a, b),
             ).start()
+
+    def keep(sent, held, recv, chunk):
         pltpu.make_async_copy(
             tile(sent, chunk, me), tile(held, chunk, me), recv.at[chunk]
         ).start()
 
     def arrived(held, send, recv, chunk):
-        spot = held.at[chunk]
-        remote(spot, spot, send.at[chunk], recv.at[chunk], (outer, inner)).wait_recv()
+        both = held.at[chunk]
+        remote(both, both, send.at[chunk], recv.at[chunk], (outer, inner)).wait_recv()
 
     def left(sent, send, recv, chunk):
-        spot = sent.at[chunk, pl.ds(0, (n_all - 1) * 8), :]
-        remote(spot, spot, send.at[chunk], recv.at[chunk], (outer, inner)).wait_send()
+        both = sent.at[chunk, pl.ds(0, (n_all - 1) * 8), :]
+        remote(both, both, send.at[chunk], recv.at[chunk], (outer, inner)).wait_send()
 
     top = dim // 2
     fetch(1).wait()
@@ -455,9 +465,9 @@
     real, imag = gates[3, 0], gates[3, 1]
     low = []
     for high in range(2):
-        spot = slice(high * top, (high + 1) * top)
-        low.append(jnp.concatenate([real[spot], -imag[spot]], axis=1))
-        low.append(jnp.concatenate([imag[spot], real[spot]], axis=1))
+        rows = slice(high * top, (high + 1) * top)
+        low.append(jnp.concatenate([real[rows], -imag[rows]], axis=1))
+        low.append(jnp.concatenate([imag[rows], real[rows]], axis=1))
     low = halves(jnp.concatenate(low, axis=0))
     fetch(0).wait()
     for chunk in range(chunks):
@@ -473,9 +483,12 @@
         names = rename(names, "b12", "b5")
         tiles = swap(tiles, names, "b11", dim // 8)
         sent_a[chunk] = join(tiles)
-        if chunk == 0:
-            pl.semaphore_wait(barrier, n_all - 1)
-        trade(sent_a, held_a, send_a, recv_a, chunk)
+        keep(sent_a, held_a, recv_a, chunk)
+        if chunk > 0:
+            trade(sent_a, held_a, send_a, recv_a, chunk, order)
+            continue
+        pl.semaphore_wait(barrier, n_all - 1)
+        trade(sent_a, held_a, send_a, recv_a, chunk, order)
 
     fetch(2).wait()
     second = complex_matrix(gates[1, 0], gates[1, 1])
@@ -510,12 +523,13 @@
             tiles = swap(tiles, names, name, dim // lane)
             names = rename(names, name, new)
         sent_b[chunk] = join(relabel(tiles, names, o_names + i_names))
-        trade(sent_b, held_b, send_b, recv_b, chunk)
+        trade(sent_b, held_b, send_b, recv_b, chunk, order)
+        keep(sent_b, held_b, recv_b, chunk)
 
     for chunk in range(chunks):
         left(sent_a, send_a, recv_a, chunk)
-    everyone = sums.at[pl.ds(0, n_all - 1)]
-    remote(everyone, everyone, send_s, recv_s, (outer, inner)).wait()
+    others = sums.at[pl.ds(0, n_all - 1)]
+    remote(others, others, send_s, recv_s, (outer, inner)).wait()
     pltpu.make_async_copy(part, sums.at[me], own_s).wait()
     for chunk in range(chunks):
         arrived(held_b, send_b, recv_b, chunk)
@@ -536,10 +550,10 @@
             tiles = swap(tiles, names, name, dim // lane)
             names = rename(names, name, new)
         tiles = relabel(tiles, names, ["c", "b13", "b12", "b11", "b7"])
-        for at in range(len(tiles)):
-            c, rest = divmod(at, len(tiles) // 2)
-            start = chunk * half + rest // 2 * 16 + rest % 2
-            out[c, pl.ds(start, 8, stride=2), :] = tiles[at] * scale
+        for c in range(2):
+            for rest in range(len(tiles) // 2):
+                start = chunk * half + rest // 2 * 16 + rest % 2
+                out[c, pl.ds(start, 8, stride=2), :] = tiles[c * len(tiles) // 2 + rest] * scale
 
 
 def fast_shards(n_outer, n_inner, state_vector, gate_matrices):

time: 24.5 us -> 23.6 us (0.963)
  Pallas kernels: 23.7 us -> 22.9 us
    pallas_call x1, Pallas kernels: 22.6 us -> 21.8 us  [fast_shards(): pl.pallas_call(functools.partial(fast_kernel, n_outer, n_inner), out_shap...]
where the time goes in v2:
time: 23.6 us; the launch traced here: 23.5 us
  Pallas kernels  22.9 us (97%)
  between operations  0.64 us (3%)
    pallas_call x1, Pallas kernels, fast_shards(): pl.pallas_call(functools.partial(fast_kernel, n_outer, n_inner), out_shap...  21.8 us
    pallas_call x1, Pallas kernels, fast_shards(): pl.pallas_call(functools.partial(fast_finish, n_all), out_shape=(jax.Shap...  1.1 us

profile of v2, /device:TPU:0, one launch (start us, length us, event | category | flops | bytes accessed | tf_op | source)
XLA Modules:
  0.0 23.5 jit_solution(16897109376397177435)
XLA Ops:
  0.6 21.8 %shard_map.41 = (f32[2,256,128]{2,1,0:T(8,128)S(1)}, f32[32,1,128]{2,1,0:T(1,128)S(1)}) custom-call(f32[2,256,128]{2,1,0:T(8,128)} %bitcast.3, f32[4,2,128,128]{3,2,1,0:T(8,128)} %gates_in.1), custom_call_target="tpu_custom_call" | custom-call | tf_op jit(solution)/shard_map/pallas_call | solution.py:569
  22.4 1.1 %shard_map.42 = (f32[2,256,128]{2,1,0:T(8,128)}, f32[1,1]{1,0:T(1,128)}) custom-call(f32[2,256,128]{2,1,0:T(8,128)S(1)} %get-tuple-element.6.values, f32[32,1,128]{2,1,0:T(1,128)S(1)} %get-tuple-element.7.sums), custom_call_target="tpu_custom_call" | custom-call | tf_op jit(solution)/shard_map/pallas_call | solution.py:589

commit v3 on v2

--- a/solution.py
+++ b/solution.py
@@ -340,20 +340,55 @@
     return picked
 
 
+def lane_bit(size, lane):
+    return lax.broadcasted_iota(jnp.int32, (8, size), 1) // lane % 2 == 1
+
+
 def swap(tiles, names, major, lane):
     step = 1 << (len(names) - 1 - names.index(major))
-    lows = [at for at in range(len(tiles)) if not at & step]
-    low = jnp.concatenate([tiles[at] for at in lows], axis=0)
-    high = jnp.concatenate([tiles[at + step] for at in lows], axis=0)
-    size = low.shape[1]
-    first = lax.broadcasted_iota(jnp.int32, low.shape, 1) // lane % 2 == 0
-    new_low = jnp.where(first, low, pltpu.roll(high, lane, 1))
-    new_high = jnp.where(first, pltpu.roll(low, size - lane, 1), high)
+    size = tiles[0].shape[1]
+    second = lane_bit(size, lane)
     out = list(tiles)
-    for j, at in enumerate(lows):
-        out[at] = new_low[j * 8 : (j + 1) * 8]
-        out[at + step] = new_high[j * 8 : (j + 1) * 8]
+    for at in range(len(tiles)):
+        if not at & step:
+            low, high = tiles[at], tiles[at + step]
+            out[at] = jnp.where(second, pltpu.roll(high, lane, 1), low)
+            out[at + step] = jnp.where(second, high, pltpu.roll(low, size - lane, 1))
     return out
+
+
+def turn(tiles, names, majors, rolled=False, roll=True):
+    count, size = len(majors), tiles[0].shape[1]
+    many, group = 1 << count, size >> count
+    steps = [1 << (len(names) - 1 - names.index(name)) for name in majors]
+    places = [
+        sum(step for j, step in enumerate(steps) if at >> (count - 1 - j) & 1)
+        for at in range(many)
+    ]
+    picks = [lane_bit(size, group << j) for j in range(count)]
+    out = list(tiles)
+    for base in range(len(tiles)):
+        if base & sum(steps):
+            continue
+        held = [tiles[base + place] for place in places]
+        if not rolled:
+            held = [held[0]] + [pltpu.roll(held[j], j * group, 1) for j in range(1, many)]
+        held = [held[-j % many] for j in range(many)]
+        for j, pick in enumerate(picks):
+            held = [jnp.where(pick, held[(at - 2**j) % many], held[at]) for at in range(many)]
+        for at, place in enumerate(places):
+            turned = roll and at > 0
+            out[base + place] = pltpu.roll(held[at], size - at * group, 1) if turned else held[at]
+    return out
+
+
+def wide_product(left, right):
+    def one(a, b):
+        return lax.dot_general(a, b, (((1,), (0,)), ((), ())), preferred_element_type=jnp.float32)
+
+    count = right[0].shape[1]
+    both = one(left[0], jnp.concatenate(right, axis=1))
+    return both[:, :count] + (both[:, count:] + one(left[1], right[0]))
 
 
 def split(values):
@@ -479,10 +514,12 @@
         wide = product(halves(wide), low, ((1,), (1,)))
         tiles = split(jnp.concatenate([wide[:, :dim], wide[:, dim:]], axis=0))
         names = ["b6", "b13", "b7", "b12", "b11"]
-        tiles = swap(tiles, names, "b12", dim // 4)
-        names = rename(names, "b12", "b5")
-        tiles = swap(tiles, names, "b11", dim // 8)
-        sent_a[chunk] = join(tiles)
+        tiles = swap(tiles, names, "b11", dim // 4)
+        names = rename(names, "b11", "b5")
+        tiles = swap(tiles, names, "b12", dim // 8)
+        names = rename(names, "b12", "b4")
+        tiles = relabel(tiles, names, ["b6", "b13", "b7", "b5", "b4"])
+        sent_a[chunk] = pltpu.roll(join(tiles), inner * (dim // n_inner), 1)
         keep(sent_a, held_a, recv_a, chunk)
         if chunk > 0:
             trade(sent_a, held_a, send_a, recv_a, chunk, order)
@@ -498,30 +535,22 @@
     total = jnp.zeros((1, dim), jnp.float32)
     for chunk in range(chunks):
         arrived(held_a, send_a, recv_a, chunk)
-        tiles = split(held_a[chunk])
-        names = o_names + i_names
-        tiles = swap(tiles, names, "i1", dim // 2)
-        names = rename(names, "i1", "c")
-        tiles = swap(tiles, names, "i0", dim // 8)
-        names = rename(names, "i0", "b11")
+        tiles = turn(split(held_a[chunk]), o_names + i_names, i_names, rolled=True)
+        names = o_names + ["c", "b11"]
         rows = ["c"] + o_names + ["b11"]
-        values = product(second, halves(join(relabel(tiles, names, rows))), ((1,), (0,)))
-        tiles, names = split(values), rows
-        for name, new, lane in (("o2", "i1", 2), ("o1", "b12", 4), ("o0", "i0", 8)):
-            tiles = swap(tiles, names, name, dim // lane)
-            names = rename(names, name, new)
+        values = wide_product(second, halves(join(relabel(tiles, names, rows))))
+        tiles = turn(split(values), rows, o_names)
+        names = ["c"] + i_names + ["b12", "b11"]
         rows = ["c"] + i_names + ["b12", "b11"]
-        values = product(third, halves(join(relabel(tiles, names, rows))), ((1,), (0,)))
+        values = wide_product(third, halves(join(relabel(tiles, names, rows))))
         total = total + jnp.sum(values * values, axis=0, keepdims=True)
         if chunk == chunks - 1:
             part[...] = total
             for k in order:
                 remote(part, sums.at[me], send_s, recv_s, peer(k)).start()
             pltpu.make_async_copy(part, sums.at[me], own_s).start()
-        tiles, names = split(values), rows
-        for name, new, lane in (("c", "o2", 2), ("b12", "o1", 4), ("b11", "o0", 8)):
-            tiles = swap(tiles, names, name, dim // lane)
-            names = rename(names, name, new)
+        tiles = turn(split(values), rows, ["c", "b11", "b12"], roll=False)
+        names = ["o2"] + i_names + ["o0", "o1"]
         sent_b[chunk] = join(relabel(tiles, names, o_names + i_names))
         trade(sent_b, held_b, send_b, recv_b, chunk, order)
         keep(sent_b, held_b, recv_b, chunk)
@@ -543,12 +572,16 @@
     root = jnp.sqrt(whole / (n_all * chunks * half * dim))
     rms[...] = root
     scale = jnp.broadcast_to(1.0 / root, (8, dim))
-    for chunk in range(chunks):
+    outer = lax.axis_index("outer")
+    turned = [(dim + (j - outer) * (dim // 8)) % dim for j in range(8)]
+    for chunk in range(chunks):
+        names = ["b6", "b13", "b7", "b5", "b4"]
         tiles = split(values[chunk])
-        names = ["b6", "b13", "b7", "b5", "b4"]
-        for name, new, lane in (("b6", "c", 2), ("b5", "b12", 4), ("b4", "b11", 8)):
-            tiles = swap(tiles, names, name, dim // lane)
-            names = rename(names, name, new)
+        for at in range(len(tiles)):
+            ahead = 4 * (at >> 4) + (at & 3)
+            tiles[at] = pltpu.roll(tiles[at], turned[ahead], 1)
+        tiles = turn(tiles, names, ["b6", "b5", "b4"], rolled=True)
+        names = ["c", "b13", "b7", "b11", "b12"]
         tiles = relabel(tiles, names, ["c", "b13", "b12", "b11", "b7"])
         for c in range(2):
             for rest in range(len(tiles) // 2):

time: 23.6 us -> 22.9 us (0.970)
  Pallas kernels: 22.9 us -> 22.1 us
    pallas_call x1, Pallas kernels: 21.8 us -> 21.1 us  [fast_shards(): pl.pallas_call(functools.partial(fast_kernel, n_outer, n_inner), out_shap...]
where the time goes in v3:
time: 22.9 us; the launch traced here: 22.8 us
  Pallas kernels  22.1 us (97%)
  between operations  0.64 us (3%)
    pallas_call x1, Pallas kernels, fast_shards(): pl.pallas_call(functools.partial(fast_kernel, n_outer, n_inner), out_shap...  21.1 us
    pallas_call x1, Pallas kernels, fast_shards(): pl.pallas_call(functools.partial(fast_finish, n_all), out_shape=(jax.Shap...  0.99 us

profile of v3, /device:TPU:0, one launch (start us, length us, event | category | flops | bytes accessed | tf_op | source)
XLA Modules:
  0.0 22.8 jit_solution(1329858376752647093)
XLA Ops:
  0.6 21.1 %shard_map.41 = (f32[2,256,128]{2,1,0:T(8,128)S(1)}, f32[32,1,128]{2,1,0:T(1,128)S(1)}) custom-call(f32[2,256,128]{2,1,0:T(8,128)} %bitcast.3, f32[4,2,128,128]{3,2,1,0:T(8,128)} %gates_in.1), custom_call_target="tpu_custom_call" | custom-call | tf_op jit(solution)/shard_map/pallas_call | solution.py:602
  21.8 1.0 %shard_map.42 = (f32[2,256,128]{2,1,0:T(8,128)}, f32[1,1]{1,0:T(1,128)}) custom-call(f32[2,256,128]{2,1,0:T(8,128)S(1)} %get-tuple-element.6.values, f32[32,1,128]{2,1,0:T(1,128)S(1)} %get-tuple-element.7.sums), custom_call_target="tpu_custom_call" | custom-call | tf_op jit(solution)/shard_map/pallas_call | solution.py:622

commit v4 on v3

--- a/solution.py
+++ b/solution.py
@@ -408,9 +408,9 @@
 
 
 def fast_kernel(
-    n_outer, n_inner, state_in, gates_in, held_b, sums,
-    state, gates, sent_a, held_a, sent_b, part, fetched,
-    send_a, recv_a, send_b, recv_b, send_s, recv_s, own_s,
+    n_outer, n_inner, state_in, gates_in, early, last, scales,
+    state, gates, sent_a, held_a, sent_b, landed, settled, part, sums, scaled, fetched,
+    send_a, recv_a, send_b, recv_b, send_s, recv_s, own_s, moved,
 ):
     def fetch(at):
         if at == 0:
@@ -446,6 +446,8 @@
     across = [(j, p) for j in range(span) for p in spots]
     beside = [(j, p) for j in reversed(range(span, levels)) for p in spots][:-1]
     order = [k for both in zip(across, beside) for k in both] + across[-1:]
+    inward = sorted(beside, key=lambda k: k[0])
+    opening = [k for both in zip(across, inward) for k in both] + across[-1:]
     barrier = pltpu.get_barrier_semaphore()
     for k in across + beside:
         pl.semaphore_signal(barrier, inc=1, device_id=peer(k), device_id_type=MESH)
@@ -458,28 +460,27 @@
             device_id=target, device_id_type=MESH,
         )
 
-    def tile(ref, chunk, at):
-        return ref.at[chunk, pl.ds(pl.multiple_of(at * 8, 8), 8), :]
+    def tile(ref, at):
+        return ref.at[pl.ds(pl.multiple_of(at * 8, 8), 8), :]
 
     def trade(sent, held, send, recv, chunk, peers):
         for k in peers:
             a, b = peer(k)
             remote(
-                tile(sent, chunk, a * n_inner + b), tile(held, chunk, me),
+                tile(sent, a * n_inner + b), tile(held, me),
                 send.at[chunk], recv.at[chunk], (a, b),
             ).start()
 
     def keep(sent, held, recv, chunk):
         pltpu.make_async_copy(
-            tile(sent, chunk, me), tile(held, chunk, me), recv.at[chunk]
+            tile(sent, me), tile(held, me), recv.at[chunk]
         ).start()
 
     def arrived(held, send, recv, chunk):
-        both = held.at[chunk]
-        remote(both, both, send.at[chunk], recv.at[chunk], (outer, inner)).wait_recv()
+        remote(held, held, send.at[chunk], recv.at[chunk], (outer, inner)).wait_recv()
 
     def left(sent, send, recv, chunk):
-        both = sent.at[chunk, pl.ds(0, (n_all - 1) * 8), :]
+        both = sent.at[pl.ds(0, (n_all - 1) * 8), :]
         remote(both, both, send.at[chunk], recv.at[chunk], (outer, inner)).wait_send()
 
     top = dim // 2
@@ -520,21 +521,22 @@
         names = rename(names, "b12", "b4")
         tiles = relabel(tiles, names, ["b6", "b13", "b7", "b5", "b4"])
         sent_a[chunk] = pltpu.roll(join(tiles), inner * (dim // n_inner), 1)
-        keep(sent_a, held_a, recv_a, chunk)
+        keep(sent_a.at[chunk], held_a.at[chunk], recv_a, chunk)
         if chunk > 0:
-            trade(sent_a, held_a, send_a, recv_a, chunk, order)
+            trade(sent_a.at[chunk], held_a.at[chunk], send_a, recv_a, chunk, order)
             continue
         pl.semaphore_wait(barrier, n_all - 1)
-        trade(sent_a, held_a, send_a, recv_a, chunk, order)
+        trade(sent_a.at[chunk], held_a.at[chunk], send_a, recv_a, chunk, opening)
 
     fetch(2).wait()
     second = complex_matrix(gates[1, 0], gates[1, 1])
     fetch(3).wait()
     third = complex_matrix(gates[2, 0], gates[2, 1])
     o_names, i_names = bits("o", o_bits), bits("i", i_bits)
+    home = [landed.at[chunk] for chunk in range(chunks - 1)] + [last]
     total = jnp.zeros((1, dim), jnp.float32)
     for chunk in range(chunks):
-        arrived(held_a, send_a, recv_a, chunk)
+        arrived(held_a.at[chunk], send_a, recv_a, chunk)
         tiles = turn(split(held_a[chunk]), o_names + i_names, i_names, rolled=True)
         names = o_names + ["c", "b11"]
         rows = ["c"] + o_names + ["b11"]
@@ -552,41 +554,60 @@
         tiles = turn(split(values), rows, ["c", "b11", "b12"], roll=False)
         names = ["o2"] + i_names + ["o0", "o1"]
         sent_b[chunk] = join(relabel(tiles, names, o_names + i_names))
-        trade(sent_b, held_b, send_b, recv_b, chunk, order)
-        keep(sent_b, held_b, recv_b, chunk)
-
-    for chunk in range(chunks):
-        left(sent_a, send_a, recv_a, chunk)
-    others = sums.at[pl.ds(0, n_all - 1)]
-    remote(others, others, send_s, recv_s, (outer, inner)).wait()
+        peers = order if chunk == chunks - 1 else across + beside
+        trade(sent_b.at[chunk], home[chunk], send_b, recv_b, chunk, peers)
+        keep(sent_b.at[chunk], home[chunk], recv_b, chunk)
+
+    moves = []
+    for chunk in range(chunks - 1):
+        arrived(home[chunk], send_b, recv_b, chunk)
+        settle(landed[chunk], outer, settled.at[chunk], None)
+        moves.append(pltpu.make_async_copy(settled.at[chunk], early.at[chunk], moved.at[chunk]))
+        moves[-1].start()
+    everyone = sums.at[pl.ds(0, n_all - 1)]
+    remote(everyone, everyone, send_s, recv_s, (outer, inner)).wait()
     pltpu.make_async_copy(part, sums.at[me], own_s).wait()
-    for chunk in range(chunks):
-        arrived(held_b, send_b, recv_b, chunk)
-        left(sent_b, send_b, recv_b, chunk)
-
-
-def fast_finish(n_all, values, sums, out, rms):
-    chunks, rows, dim = values.shape
-    half = rows // 2
     whole = jnp.sum(jnp.sum(sums[...], axis=0), axis=1, keepdims=True)
-    root = jnp.sqrt(whole / (n_all * chunks * half * dim))
-    rms[...] = root
-    scale = jnp.broadcast_to(1.0 / root, (8, dim))
+    root = jnp.sqrt(whole / (n_all * chunks * dim * dim))
+    scaled[:8, :] = jnp.broadcast_to(1.0 / root, (8, dim))
+    scaled[8:, :] = jnp.broadcast_to(root, (8, dim))
+    moves.append(pltpu.make_async_copy(scaled, scales, moved.at[chunks - 1]))
+    moves[-1].start()
+    for chunk in range(chunks):
+        left(sent_a.at[chunk], send_a, recv_a, chunk)
+    for move in moves:
+        move.wait()
+    for chunk in range(chunks):
+        left(sent_b.at[chunk], send_b, recv_b, chunk)
+    arrived(last, send_b, recv_b, chunks - 1)
+
+
+def settle(values, outer, out, scale):
+    size = values.shape[1]
+    ahead = [(size + (j - outer) * (size // 8)) % size for j in range(8)]
+    tiles = split(values)
+    for at in range(len(tiles)):
+        tiles[at] = pltpu.roll(tiles[at], ahead[4 * (at >> 4) + (at & 3)], 1)
+    names = ["b6", "b13", "b7", "b5", "b4"]
+    tiles = turn(tiles, names, ["b6", "b5", "b4"], rolled=True)
+    names = ["c", "b13", "b7", "b11", "b12"]
+    tiles = relabel(tiles, names, ["c", "b13", "b12", "b11", "b7"])
+    for at in range(len(tiles)):
+        c, rest = divmod(at, len(tiles) // 2)
+        kept = tiles[at] if scale is None else tiles[at] * scale
+        out[c, pl.ds(rest // 2 * 16 + rest % 2, 8, stride=2), :] = kept
+
+
+def fast_finish(early, last, scales, out, rms):
+    count, _, half, dim = early.shape
+    scale = scales[:8, :]
+    rms[...] = scales[8:9, :1]
+    for chunk in range(count):
+        for c in range(2):
+            values = early[chunk, c].reshape(-1, 8, dim) * scale[None]
+            out[c, chunk * half : (chunk + 1) * half, :] = values.reshape(half, dim)
     outer = lax.axis_index("outer")
-    turned = [(dim + (j - outer) * (dim // 8)) % dim for j in range(8)]
-    for chunk in range(chunks):
-        names = ["b6", "b13", "b7", "b5", "b4"]
-        tiles = split(values[chunk])
-        for at in range(len(tiles)):
-            ahead = 4 * (at >> 4) + (at & 3)
-            tiles[at] = pltpu.roll(tiles[at], turned[ahead], 1)
-        tiles = turn(tiles, names, ["b6", "b5", "b4"], rolled=True)
-        names = ["c", "b13", "b7", "b11", "b12"]
-        tiles = relabel(tiles, names, ["c", "b13", "b12", "b11", "b7"])
-        for c in range(2):
-            for rest in range(len(tiles) // 2):
-                start = chunk * half + rest // 2 * 16 + rest % 2
-                out[c, pl.ds(start, 8, stride=2), :] = tiles[c * len(tiles) // 2 + rest] * scale
+    settle(last[...], outer, out.at[:, pl.ds(count * half, half), :], scale)
 
 
 def fast_shards(n_outer, n_inner, state_vector, gate_matrices):
@@ -599,36 +620,41 @@
     vmem = pl.BlockSpec(memory_space=pltpu.VMEM)
     hbm = pl.BlockSpec(memory_space=pltpu.HBM)
     anywhere = pl.BlockSpec(memory_space=pl.ANY)
-    values, sums = pl.pallas_call(
+    early = (chunks - 1, 2, dim, dim)
+    held_values = pl.pallas_call(
         functools.partial(fast_kernel, n_outer, n_inner),
         out_shape=(
-            jax.ShapeDtypeStruct((chunks, n_all * 8, dim), jnp.float32),
-            jax.ShapeDtypeStruct((n_all, 1, dim), jnp.float32),
+            jax.ShapeDtypeStruct(early, jnp.float32),
+            jax.ShapeDtypeStruct((n_all * 8, dim), jnp.float32),
+            jax.ShapeDtypeStruct((16, dim), jnp.float32),
         ),
         in_specs=[hbm, hbm],
-        out_specs=(anywhere, anywhere),
+        out_specs=(anywhere, anywhere, anywhere),
         scratch_shapes=[
             pltpu.VMEM((2, rows, dim), jnp.float32),
             pltpu.VMEM(gate_matrices.shape, jnp.float32),
         ]
         + [held] * 3
-        + [pltpu.VMEM((1, dim), jnp.float32), dma((5,))]
+        + [pltpu.VMEM((chunks - 1, n_all * 8, dim), jnp.float32), pltpu.VMEM(early, jnp.float32)]
+        + [pltpu.VMEM(shape, jnp.float32) for shape in ((1, dim), (n_all, 1, dim), (16, dim))]
+        + [dma((5,))]
         + [dma((chunks,))] * 4
-        + [dma(())] * 3,
+        + [dma(())] * 3
+        + [dma((chunks,))],
         compiler_params=pltpu.CompilerParams(
             collective_id=0, has_side_effects=True, vmem_limit_bytes=TRADE_LIMIT
         ),
     )(state_vector.reshape(2, rows, dim), gate_matrices)
     final_state, root = pl.pallas_call(
-        functools.partial(fast_finish, n_all),
+        fast_finish,
         out_shape=(
             jax.ShapeDtypeStruct((2, rows, dim), jnp.float32),
             jax.ShapeDtypeStruct((1, 1), jnp.float32),
         ),
-        in_specs=[vmem, vmem],
+        in_specs=[vmem, vmem, vmem],
         out_specs=(vmem, vmem),
         compiler_params=pltpu.CompilerParams(vmem_limit_bytes=LIMIT),
-    )(values, sums)
+    )(*held_values)
     return final_state.reshape(state_vector.shape), root.reshape(())
 
 

time: 22.9 us -> 22.4 us (0.978)
  Pallas kernels: 22.1 us -> 21.7 us
    pallas_call x1, Pallas kernels: 21.1 us -> 20.7 us  [fast_shards(): pl.pallas_call(functools.partial(fast_kernel, n_outer, n_inner), out_shap...]
where the time goes in v4:
time: 22.4 us; the launch traced here: 22.3 us
  Pallas kernels  21.7 us (97%)
  between operations  0.64 us (3%)
    pallas_call x1, Pallas kernels, fast_shards(): pl.pallas_call(functools.partial(fast_kernel, n_outer, n_inner), out_shap...  20.7 us
    pallas_call x1, Pallas kernels, fast_shards(): pl.pallas_call(fast_finish, out_shape=(jax.ShapeDtypeStruct((2, rows, dim...  0.91 us

profile of v4, /device:TPU:0, one launch (start us, length us, event | category | flops | bytes accessed | tf_op | source)
XLA Modules:
  0.0 22.3 jit_solution(11517439089362655255)
XLA Ops:
  0.6 20.7 %shard_map.41 = (f32[1,2,128,128]{3,2,1,0:T(8,128)S(1)}, f32[256,128]{1,0:T(8,128)S(1)}, f32[16,128]{1,0:T(8,128)S(1)}) custom-call(f32[2,256,128]{2,1,0:T(8,128)} %bitcast.3, f32[4,2,128,128]{3,2,1,0:T(8,128)} %gates_in.1), custom_call_target="tpu_custom_call" | custom-call | tf_op jit(solution)/shard_map/pallas_call | solution.py:624
  21.4 0.9 %shard_map.42 = (f32[2,256,128]{2,1,0:T(8,128)}, f32[1,1]{1,0:T(1,128)}) custom-call(f32[1,2,128,128]{3,2,1,0:T(8,128)S(1)} %get-tuple-element.7.early, f32[256,128]{1,0:T(8,128)S(1)} %get-tuple-element.8.last, f32[16,128]{1,0:T(8,128)S(1)} %get-tuple-element.9.scales), custom_call_target="tpu_custom_call" | custom-call | tf_op jit(solution)/shard_map/pallas_call | solution.py:648

commit v5 on v4

--- a/solution.py
+++ b/solution.py
@@ -555,8 +555,8 @@
         names = ["o2"] + i_names + ["o0", "o1"]
         sent_b[chunk] = join(relabel(tiles, names, o_names + i_names))
         peers = order if chunk == chunks - 1 else across + beside
+        keep(sent_b.at[chunk], home[chunk], recv_b, chunk)
         trade(sent_b.at[chunk], home[chunk], send_b, recv_b, chunk, peers)
-        keep(sent_b.at[chunk], home[chunk], recv_b, chunk)
 
     moves = []
     for chunk in range(chunks - 1):

time: 22.4 us -> 22.4 us (level)
  no operation moved by 1% of the time
where the time goes in v5:
time: 22.4 us; the launch traced here: 22.3 us
  Pallas kernels  21.7 us (97%)
  between operations  0.64 us (3%)
    pallas_call x1, Pallas kernels, fast_shards(): pl.pallas_call(functools.partial(fast_kernel, n_outer, n_inner), out_shap...  20.7 us
    pallas_call x1, Pallas kernels, fast_shards(): pl.pallas_call(fast_finish, out_shape=(jax.ShapeDtypeStruct((2, rows, dim...  0.91 us

profile of v5, /device:TPU:0, one launch (start us, length us, event | category | flops | bytes accessed | tf_op | source)
XLA Modules:
  0.0 22.3 jit_solution(1688629586807972366)
XLA Ops:
  0.6 20.7 %shard_map.41 = (f32[1,2,128,128]{3,2,1,0:T(8,128)S(1)}, f32[256,128]{1,0:T(8,128)S(1)}, f32[16,128]{1,0:T(8,128)S(1)}) custom-call(f32[2,256,128]{2,1,0:T(8,128)} %bitcast.3, f32[4,2,128,128]{3,2,1,0:T(8,128)} %gates_in.1), custom_call_target="tpu_custom_call" | custom-call | tf_op jit(solution)/shard_map/pallas_call | solution.py:624
  21.4 0.9 %shard_map.42 = (f32[2,256,128]{2,1,0:T(8,128)}, f32[1,1]{1,0:T(1,128)}) custom-call(f32[1,2,128,128]{3,2,1,0:T(8,128)S(1)} %get-tuple-element.7.early, f32[256,128]{1,0:T(8,128)S(1)} %get-tuple-element.8.last, f32[16,128]{1,0:T(8,128)S(1)} %get-tuple-element.9.scales), custom_call_target="tpu_custom_call" | custom-call | tf_op jit(solution)/shard_map/pallas_call | solution.py:648
